TPU v7x, 128 devices: a whole 4x4x4 slice. The times are simulated.
128 devices in a mesh: row: 32 (over y_lo, z, x), col: 4 (over y_hi, core).
Axes of the slice: x: 4, y: 4 (y_hi: 2, y_lo: 2; y = y_hi * 2 + y_lo), z: 4, core: 2. Of those that a mesh axis runs over, the one named last changes fastest.
Arguments:
- flow: bfloat16 [8192, 8192], P('row', 'col'), may hold values from 0.0009994507 to 1
- pattern: int32 [32, 32], P('row', 'col'), may hold values 0 or 1
- keep: int32 [32, 32], P('row', 'col'), may hold values 0 or 1
Outputs:
- clustered: float32 [8192, 8192], P('row', 'col')
All inputs are finite; a program needn't handle non-finite values. No bound on the sum of `pattern` or of `keep` on one device may be relied on, other than what follows from the above.
Results may differ from a plain program's by a relative error of at most 0.00046.
Values may be sent and summed in bfloat16 or wider, within the bound.
A program may use at most 128 MiB of HBM per device.

v0:
```python
import jax
import jax.numpy as jnp
from jax import lax
from jax.sharding import PartitionSpec as P


def spread_tiles(grid, tile):
    trows, tcols = grid.shape
    wide = jnp.broadcast_to(grid[:, None, :, None], (trows, tile, tcols, tile))
    return wide.reshape(trows * tile, tcols * tile)


def body(flow, pattern, keep):
    rows_dev, cols_dev = flow.shape
    trows, tcols = pattern.shape
    tile = rows_dev // trows
    row_start = lax.axis_index("row") * rows_dev
    col_start = lax.axis_index("col") * cols_dev
    global_rows = row_start + lax.iota(jnp.int32, rows_dev)
    global_cols = col_start + lax.iota(jnp.int32, cols_dev)
    loops = (global_rows[:, None] == global_cols[None, :]).astype(jnp.float32)
    base = flow.astype(jnp.float32) * spread_tiles((pattern > 0).astype(jnp.float32), tile) + loops
    mass = lax.psum(jnp.sum(base, axis=0), "row")
    stochastic = (base / mass[None, :]).astype(jnp.bfloat16)
    left = lax.all_gather(stochastic, "col", axis=1, tiled=True)
    right = lax.all_gather(stochastic, "row", axis=0, tiled=True)
    expanded = jnp.dot(left, right, preferred_element_type=jnp.float32)
    tile_rows = lax.axis_index("row") * trows + lax.iota(jnp.int32, trows)
    tile_cols = lax.axis_index("col") * tcols + lax.iota(jnp.int32, tcols)
    kept = jnp.logical_or(keep > 0, tile_rows[:, None] == tile_cols[None, :]).astype(jnp.float32)
    expanded = expanded * spread_tiles(kept, tile)
    inflated = expanded * expanded
    partial_totals = jnp.sum(inflated, axis=0)
    order = rows_dev * lax.axis_size("row")
    totals = lax.psum(partial_totals, "row")
    scale = order / totals
    return inflated * scale[None, :]


def solution(mesh):
    return jax.shard_map(
        body,
        mesh=mesh,
        in_specs=(P("row", "col"), P("row", "col"), P("row", "col")),
        out_specs=P("row", "col"),
        check_vma=False,
    )
```

profile of v0, /device:TPU:0, one launch (start us, length us, event | category | flops | bytes accessed | tf_op | source)
XLA Modules:
  0.0 601.0 jit_solution(7701374311171810818)
XLA Ops:
  6.5 0.0 all-gather.3.cloned.1.call-start
  6.5 0.7 fusion.2
  7.2 0.1 broadcast_bitcast_fusion.1
  7.3 1.7 fusion.1
  9.0 85.2 %psum.14 = f32[2048]{0:T(1024)S(1)} all-reduce(f32[2048]{0:T(1024)S(1)} %fusion.1), channel_id=1, replica_groups=mesh['row'=32,'col'=4] {'row'}, use_global_device_ids=true, to_apply=%region_1.0 | all-reduce | flops 2048 | bytes 16384 | tf_op jit(solution)/shard_map/psum | solution.py:23
  94.2 0.0 copy-start
  94.2 2.7 divide_convert_fusion
  96.9 0.0 all-gather.3.cloned.1.call-update
  96.9 0.0 all-gather.5.cloned.1.call-start
  97.0 0.7 all-gather.5.cloned.1.call-update
  97.7 0.0 copy-done
  97.7 0.1 broadcast_bitcast_fusion
  97.8 34.0 %all-gather.3.cloned.1.call-done = bf16[256,8192]{1,0:T(8,128)(2,1)} async-done(((bf16[256,2048]{1,0:T(8,128)(2,1)}), bf16[256,8192]{1,0:T(8,128)(2,1)}) %all-gather.3.cloned.1.call-update) | async-done | bytes 4194320 | tf_op jit(solution)/shard_map/all_gather | solution.py:25
  131.7 365.9 %all-gather.5.cloned.1.call-done = bf16[8192,2048]{1,0:T(8,128)(2,1)} async-done(((bf16[256,2048]{1,0:T(8,128)(2,1)}), bf16[8192,2048]{1,0:T(8,128)(2,1)}) %all-gather.5.cloned.1.call-update) | async-done | bytes 33554448 | tf_op jit(solution)/shard_map/all_gather | solution.py:26
  497.6 16.3 %fusion.4 = (f32[2048]{0:T(1024)S(1)}, f32[256,2048]{1,0:T(8,128)S(1)}) fusion(f32[2048]{0:T(1024)S(1)} %bitcast.14, bf16[256,8192]{1,0:T(8,128)(2,1)} %all-gather.3.cloned.1.call-done, bf16[8192,2048]{1,0:T(8,128)(2,1)} %all-gather.5.cloned.1.call-done), kind=kOutput, calls=%fused_computation.15 | convolution fusion | flops 8591505408 | bytes 39862272 | tf_op jit(solution)/shard_map/dot_general | solution.py:27
  513.9 78.7 %psum.15 = f32[2048]{0:T(1024)S(1)} all-reduce(f32[2048]{0:T(1024)S(1)} %get-tuple-element.5), channel_id=1, replica_groups=mesh['row'=32,'col'=4] {'row'}, use_global_device_ids=true, to_apply=%region_3.0 | all-reduce | flops 2048 | bytes 16384 | tf_op jit(solution)/shard_map/psum | solution.py:35
  592.6 1.6 broadcast_multiply_fusion
  (6 shorter events, 0.0 us)
Async XLA Ops:
  6.5 125.2 %all-gather.3.cloned.1.call-start = ((), (), s32[]{:S(2)}) async-start(), calls=%async_computation | async-start | bytes 5242880 | tf_op jit(solution)/shard_map/all_gather | solution.py:25
  94.2 3.5 copy-start
  96.9 400.7 %all-gather.5.cloned.1.call-start = ((), (), s32[]{:S(2)}) async-start(), calls=%async_computation.1 | async-start | bytes 34603008 | tf_op jit(solution)/shard_map/all_gather | solution.py:26
Sparse Core Ops, SparseCore 0:
  97.0 34.6 all-gather.2
  133.4 364.2 all-gather.4
where the time goes:
time: 601 us
  waiting for transfers between devices  401 us (67%)
  blocking collectives  164 us (27%)
  matrix products  16.3 us (3%)
  between operations  13.5 us (2%)
  other arithmetic  6.62 us (1%)
    all_gather x1, waiting for transfers between devices, body(): right = lax.all_gather(stochastic, 'row', axis=0, tiled=True)  366 us
    psum x1, blocking collectives, body(): mass = lax.psum(jnp.sum(base, axis=0), 'row')  85.2 us
    psum x1, blocking collectives, body(): totals = lax.psum(partial_totals, 'row')  78.7 us
    all_gather x1, waiting for transfers between devices, body(): left = lax.all_gather(stochastic, 'col', axis=1, tiled=True)  34 us
    dot_general x1, matrix products, body(): expanded = jnp.dot(left, right, preferred_element_type=jnp.float32)  16.3 us
  transfers between devices with their start and end apart: 2, of which 2 were waited for; matrix products, arithmetic and copies ran while one was open for 0% of the time, Pallas kernels for 0%

commit v1 on v0

--- a/solution.py
+++ b/solution.py
@@ -20,7 +20,7 @@
     global_cols = col_start + lax.iota(jnp.int32, cols_dev)
     loops = (global_rows[:, None] == global_cols[None, :]).astype(jnp.float32)
     base = flow.astype(jnp.float32) * spread_tiles((pattern > 0).astype(jnp.float32), tile) + loops
-    mass = lax.psum(jnp.sum(base, axis=0), "row")
+    mass = jnp.sum(lax.all_gather(jnp.sum(base, axis=0), "row"), axis=0)
     stochastic = (base / mass[None, :]).astype(jnp.bfloat16)
     left = lax.all_gather(stochastic, "col", axis=1, tiled=True)
     right = lax.all_gather(stochastic, "row", axis=0, tiled=True)

time: 601 us -> 599 us (level)
    psum x1 -> x0, blocking collectives: 85.2 us -> none  [body(): mass = lax.psum(jnp.sum(base, axis=0), 'row')]
    all_gather x0 -> x1, blocking collectives: none -> 84 us  [body(): mass = jnp.sum(lax.all_gather(jnp.sum(base, axis=0), 'row'), axis=0)]
where the time goes in v1:
time: 599 us
  waiting for transfers between devices  401 us (67%)
  blocking collectives  163 us (27%)
  matrix products  16.3 us (3%)
  between operations  13.5 us (2%)
    all_gather x1, waiting for transfers between devices, body(): right = lax.all_gather(stochastic, 'row', axis=0, tiled=True)  366 us
    all_gather x1, blocking collectives, body(): mass = jnp.sum(lax.all_gather(jnp.sum(base, axis=0), 'row'), axis=0)  84 us
    psum x1, blocking collectives, body(): totals = lax.psum(partial_totals, 'row')  78.7 us
    all_gather x1, waiting for transfers between devices, body(): left = lax.all_gather(stochastic, 'col', axis=1, tiled=True)  34 us
    dot_general x1, matrix products, body(): expanded = jnp.dot(left, right, preferred_element_type=jnp.float32)  16.3 us
  transfers between devices with their start and end apart: 2, of which 2 were waited for; matrix products, arithmetic and copies ran while one was open for 0% of the time, Pallas kernels for 0%

profile of v1, /device:TPU:0, one launch (start us, length us, event | category | flops | bytes accessed | tf_op | source)
XLA Modules:
  0.0 598.7 jit_solution(3512231451956925856)
XLA Ops:
  6.5 0.0 copy-start
  6.5 0.0 all-gather.4.cloned.1.call-start
  6.5 0.7 fusion.2
  7.3 0.1 broadcast_bitcast_fusion.1
  7.4 1.7 fusion.1
  9.1 84.0 %all-gather = f32[65536]{0:T(1024)S(1)} all-gather(f32[2048]{0:T(1024)S(1)} %fusion.1), channel_id=2, replica_groups=mesh['row'=32,'col'=4] {'row'}, dimensions={0}, use_global_device_ids=true | all-gather | bytes 270336 | tf_op jit(solution)/shard_map/all_gather | solution.py:23
  93.1 0.0 copy-done
  93.1 0.0 copy-start.1
  93.1 1.5 divide_convert_fusion
  94.6 0.0 all-gather.4.cloned.1.call-update
  94.6 0.0 all-gather.6.cloned.1.call-start
  94.7 0.7 all-gather.6.cloned.1.call-update
  95.4 0.0 copy-done.1
  95.4 0.1 broadcast_bitcast_fusion
  95.5 34.0 %all-gather.4.cloned.1.call-done = bf16[256,8192]{1,0:T(8,128)(2,1)} async-done(((bf16[256,2048]{1,0:T(8,128)(2,1)}), bf16[256,8192]{1,0:T(8,128)(2,1)}) %all-gather.4.cloned.1.call-update) | async-done | bytes 4194320 | tf_op jit(solution)/shard_map/all_gather | solution.py:25
  129.5 365.9 %all-gather.6.cloned.1.call-done = bf16[8192,2048]{1,0:T(8,128)(2,1)} async-done(((bf16[256,2048]{1,0:T(8,128)(2,1)}), bf16[8192,2048]{1,0:T(8,128)(2,1)}) %all-gather.6.cloned.1.call-update) | async-done | bytes 33554448 | tf_op jit(solution)/shard_map/all_gather | solution.py:26
  495.4 16.3 %fusion.4 = (f32[2048]{0:T(1024)S(1)}, f32[256,2048]{1,0:T(8,128)S(1)}) fusion(f32[2048]{0:T(1024)S(1)} %bitcast.14, bf16[256,8192]{1,0:T(8,128)(2,1)} %all-gather.4.cloned.1.call-done, bf16[8192,2048]{1,0:T(8,128)(2,1)} %all-gather.6.cloned.1.call-done), kind=kOutput, calls=%fused_computation.15 | convolution fusion | flops 8591505408 | bytes 39862272 | tf_op jit(solution)/shard_map/dot_general | solution.py:27
  511.6 78.7 %psum.7 = f32[2048]{0:T(1024)S(1)} all-reduce(f32[2048]{0:T(1024)S(1)} %get-tuple-element.5), channel_id=1, replica_groups=mesh['row'=32,'col'=4] {'row'}, use_global_device_ids=true, to_apply=%region_3.0 | all-reduce | flops 2048 | bytes 16384 | tf_op jit(solution)/shard_map/psum | solution.py:35
  590.3 1.6 broadcast_multiply_fusion
  (8 shorter events, 0.1 us)
Async XLA Ops:
  6.5 86.6 %copy-start = (bf16[256,2048]{1,0:T(8,128)(2,1)S(1)}, bf16[256,2048]{1,0:T(8,128)(2,1)}, u32[]{:S(2)}) copy-start(bf16[256,2048]{1,0:T(8,128)(2,1)} %param.3) | copy-start | bytes 3145732
  6.5 122.9 %all-gather.4.cloned.1.call-start = ((), (), s32[]{:S(2)}) async-start(), calls=%async_computation | async-start | bytes 5242880 | tf_op jit(solution)/shard_map/all_gather | solution.py:25
  93.1 2.3 copy-start.1
  94.6 400.7 %all-gather.6.cloned.1.call-start = ((), (), s32[]{:S(2)}) async-start(), calls=%async_computation.1 | async-start | bytes 34603008 | tf_op jit(solution)/shard_map/all_gather | solution.py:26
Sparse Core Ops, SparseCore 0:
  94.7 34.6 all-gather.3
  131.1 364.2 all-gather.5
